TPU v7x, 512 devices: a whole 4x8x8 slice. The times are simulated.
512 devices in a mesh: gs: 128 (over y, z, core), view: 4 (over x).
Axes of the slice: x: 4, y: 8, z: 8, core: 2. Of those that a mesh axis runs over, the one named last changes fastest.
Arguments:
- features: bfloat16 [131072, 128], P('gs'), may hold values from -6 to 6
- geometry: float32 [4, 9, 131072], P('view', None, 'gs'), as said below
- decoder: bfloat16 [128, 512], replicated, may hold values from -0.5 to 0.5
- teacher: bfloat16 [4, 131072, 512], P('view', 'gs'), may hold values from -3 to 3
- images: float32 [4, 3, 131072], P('view', None, 'gs'), may hold values from 0 to 1
- send_index: int32 [4, 128, 1024], P('view', 'gs'), may hold values from 0 to 1023, as said below
- tile_lists: int32 [4, 512, 8], P('view', 'gs'), may hold values from 0 to 7, as said below
- tile_lengths: int32 [4, 512], P('view', 'gs'), may hold values from 2 to 8
Outputs:
- feature_grad: float32 [131072, 128], P(('gs', 'view'))
- geometry_grad: float32 [4, 9, 131072], P('view', None, 'gs')
- decoder_grad: float32 [128, 512], replicated
Inputs may be any that keep to these rules, and one draw needn't show every extreme that they name: `send_index`: each row (one view, one source device) is a permutation of 0 .. 1023; positions k * 8 to (k + 1) * 8 - 1 hold the Gaussians sent to the device of gs index k. `tile_lists`: the 8 entries of a row are distinct. `geometry`: opacity logits lie in -7.5 .. -4, log conics between -2 log 16 and -2 log 16 + 2 log 4, shears in -2 .. 2, colors in 0 .. 1.
All inputs are finite; a program needn't handle non-finite values.
Results may differ from a plain program's by a relative error of at most 0.0017.
Values may be sent and summed in bfloat16 or wider, within the bound.
A program may use at most 64 MiB of HBM per device.

v0:
```python
import math
import jax
import jax.numpy as jnp
from jax import lax
from jax.sharding import PartitionSpec as P

FEAT = 128
CT = 512
TS = 16
BLK = 128
LIST = 8


def composite(tile_geo, alive_mask, pixel_x, pixel_y):
    delta_x = pixel_x[:, None] - tile_geo[0][None, :]
    delta_y = pixel_y[:, None] - tile_geo[1][None, :]
    conic_a = jnp.exp(tile_geo[2])
    conic_c = jnp.exp(tile_geo[3])
    conic_b = 0.8 * jnp.tanh(tile_geo[4]) * jnp.exp(0.5 * (tile_geo[2] + tile_geo[3]))
    exponent = -0.5 * (
        conic_a * delta_x * delta_x
        + 2.0 * conic_b * delta_x * delta_y
        + conic_c * delta_y * delta_y
    )
    opacity = alive_mask * jax.nn.sigmoid(tile_geo[5])
    alpha_val = opacity[None, :] * jnp.exp(exponent)
    log_keep = jnp.log1p(-alpha_val)
    pixel_count = pixel_x.shape[0]
    blocked = log_keep.reshape(pixel_count, LIST, BLK)
    inner = jnp.cumsum(blocked, axis=2) - blocked
    block_sums = jnp.sum(blocked, axis=2)
    outer = jnp.cumsum(block_sums, axis=1) - block_sums
    before = (inner + outer[:, :, None]).reshape(pixel_count, LIST * BLK)
    weights = alpha_val * jnp.exp(before)
    pixel_color = jnp.einsum("pi,ci->cp", weights, tile_geo[6:9], precision=lax.Precision.HIGHEST)
    return (weights, pixel_color)


def device_terms(
    recv_geo, recv_feat, decoder, teacher_dev, images_dev, lists, lengths, shard_index
):
    nblocks = recv_feat.shape[0] // BLK
    tile_pixels = TS * TS
    geo_blocks = recv_geo.reshape(9, nblocks, BLK)
    feat_blocks = recv_feat.reshape(nblocks, BLK, FEAT)
    within = jnp.arange(tile_pixels, dtype=jnp.int32)
    block_range = jnp.arange(nblocks, dtype=jnp.int32)
    slot_range = jnp.arange(LIST, dtype=jnp.int32)

    def tile_step(totals, tile_index):
        decoder_sum, geo_acc, feat_acc = totals
        block_ids = lists[tile_index]
        count = lengths[tile_index]
        alive_mask = jnp.broadcast_to(
            (slot_range < count).astype(jnp.float32)[:, None], (LIST, BLK)
        ).reshape(LIST * BLK)
        tile_geo = jnp.take(geo_blocks, block_ids, axis=1).reshape(9, LIST * BLK)
        feat_tile = jnp.take(feat_blocks, block_ids, axis=0).reshape(LIST * BLK, FEAT)
        column = 2 * TS * (shard_index % 30) + TS * (tile_index % 2) + within % TS
        row_index = 2 * TS * (shard_index // 30) + TS * (tile_index // 2) + within // TS
        pixel_x = column.astype(jnp.float32) + 0.5
        pixel_y = row_index.astype(jnp.float32) + 0.5
        (weights, pixel_color), pullback = jax.vjp(
            lambda geo_part: composite(geo_part, alive_mask, pixel_x, pixel_y), tile_geo
        )
        weight_b = weights.astype(jnp.bfloat16)
        rendered = jnp.dot(weight_b, feat_tile, preferred_element_type=jnp.float32).astype(
            jnp.bfloat16
        )
        pred = jnp.dot(rendered, decoder, preferred_element_type=jnp.float32)
        teacher_rows = lax.dynamic_slice_in_dim(
            teacher_dev, tile_index * tile_pixels, tile_pixels, 0
        )
        error_feat = pred - teacher_rows.astype(jnp.float32)
        gpred = (error_feat / jnp.sqrt(error_feat * error_feat + 0.04)).astype(jnp.bfloat16)
        grender = lax.dot_general(
            gpred, decoder, (((1,), (1,)), ((), ())), preferred_element_type=jnp.float32
        ).astype(jnp.bfloat16)
        decoder_sum = decoder_sum + lax.dot_general(
            rendered, gpred, (((0,), (0,)), ((), ())), preferred_element_type=jnp.float32
        )
        image_cols = lax.dynamic_slice_in_dim(images_dev, tile_index * tile_pixels, tile_pixels, 1)
        error_color = pixel_color - image_cols
        gcolor = error_color / jnp.sqrt(error_color * error_color + 0.04)
        gweight = lax.dot_general(
            grender, feat_tile, (((1,), (1,)), ((), ())), preferred_element_type=jnp.float32
        )
        gfeat_tile = lax.dot_general(
            weight_b, grender, (((0,), (0,)), ((), ())), preferred_element_type=jnp.float32
        )
        (ggeo_tile,) = pullback((gweight, gcolor))
        hits = (block_ids[:, None] == block_range[None, :]).astype(jnp.float32)
        geo_acc = geo_acc + jnp.einsum(
            "clb,ln->cnb", ggeo_tile.reshape(9, LIST, BLK), hits, precision=lax.Precision.HIGHEST
        )
        feat_acc = feat_acc + jnp.einsum(
            "ln,lbf->nbf",
            hits,
            gfeat_tile.reshape(LIST, BLK, FEAT),
            precision=lax.Precision.HIGHEST,
        )
        return ((decoder_sum, geo_acc, feat_acc), None)

    start_totals = (
        jnp.zeros((FEAT, CT), jnp.float32),
        jnp.zeros((9, nblocks, BLK), jnp.float32),
        jnp.zeros((nblocks, BLK, FEAT), jnp.float32),
    )
    tile_range = jnp.arange(lists.shape[0], dtype=jnp.int32)
    (decoder_sum, geo_acc, feat_acc), _ = lax.scan(tile_step, start_totals, tile_range)
    return (decoder_sum, geo_acc.reshape(9, nblocks * BLK), feat_acc.reshape(nblocks * BLK, FEAT))


def on_device(features, geometry, decoder, teacher, images, send_index, tile_lists, tile_lengths):
    send_order = send_index[0, 0]
    shard_index = lax.axis_index("gs")
    geo_send = jnp.take(geometry[0], send_order, axis=1)
    recv_geo = lax.all_to_all(geo_send, "gs", split_axis=1, concat_axis=1, tiled=True)
    feat_send = jnp.take(features, send_order, axis=0)
    recv_feat = lax.all_to_all(feat_send, "gs", split_axis=0, concat_axis=0, tiled=True)
    decoder_sum, geo_acc, feat_acc = device_terms(
        recv_geo,
        recv_feat,
        decoder,
        teacher[0],
        images[0],
        tile_lists[0],
        tile_lengths[0],
        shard_index,
    )
    returned_geo = lax.all_to_all(geo_acc, "gs", split_axis=1, concat_axis=1, tiled=True)
    returned_feat = lax.all_to_all(feat_acc, "gs", split_axis=0, concat_axis=0, tiled=True)
    geo_own = jnp.zeros_like(returned_geo).at[:, send_order].set(returned_geo)
    feat_own = jnp.zeros_like(returned_feat).at[send_order].set(returned_feat)
    quarter = feat_own.shape[0] // lax.axis_size("view")
    summed = lax.psum(feat_own, "view")
    feature_grad = lax.dynamic_slice_in_dim(summed, lax.axis_index("view") * quarter, quarter, 0)
    pixel_total = lax.axis_size("gs") * lax.axis_size("view") * tile_lists.shape[1] * TS * TS
    decoder_grad = lax.psum(decoder_sum, ("gs", "view")) * (1.0 / math.sqrt(pixel_total))
    return (feature_grad, geo_own[None], decoder_grad)


def solution(mesh):
    placed = (
        P("gs", None),
        P("view", None, "gs"),
        P(),
        P("view", "gs", None),
        P("view", None, "gs"),
        P("view", "gs", None),
        P("view", "gs", None),
        P("view", "gs"),
    )
    return jax.shard_map(
        on_device,
        mesh=mesh,
        in_specs=placed,
        out_specs=(P(("gs", "view"), None), P("view", None, "gs"), P()),
        check_vma=False,
    )
```

profile of v0, /device:TPU:8, one launch (start us, length us, event | category | flops | bytes accessed | tf_op | source)
XLA Modules:
  0.0 610.4 jit_solution(10011325874883574381)
XLA Ops:
  10.2 2.8 gather_fusion.2
  14.1 17.4 %all-to-all-start = ((f32[9,128,8]{0,2,1:T(8,128)}), f32[9,128,8]{0,2,1:T(8,128)S(1)}, u32[]{:S(2)}, u32[]{:S(2)}) async-start(f32[9,128,8]{0,2,1:T(8,128)} %bitcast_select_fusion.1), calls=%async_computation | async-start | bytes 1048576 | tf_op jit(solution)/shard_map/all_to_all | solution.py:118
  31.5 3.2 gather_fusion.3
  35.6 16.2 %all-to-all-done = f32[9,128,8]{0,2,1:T(8,128)S(1)} async-done(((f32[9,128,8]{0,2,1:T(8,128)}), f32[9,128,8]{0,2,1:T(8,128)S(1)}, u32[]{:S(2)}, u32[]{:S(2)}) %all-to-all-start) | async-done | bytes 36896 | tf_op jit(solution)/shard_map/all_to_all | solution.py:118
  51.8 6.5 %all-to-all-start.1 = ((bf16[128,8,128]{2,1,0:T(8,128)(2,1)}), bf16[128,8,128]{2,1,0:T(8,128)(2,1)S(1)}, u32[]{:S(2)}, u32[]{:S(2)}) async-start(bf16[128,8,128]{2,1,0:T(8,128)(2,1)} %bitcast_select_fusion.2), calls=%async_computation.1 | async-start | bytes 524288 | tf_op jit(solution)/shard_map/all_to_all | solution.py:120
  60.4 12.6 %all-to-all-done.1 = bf16[128,8,128]{2,1,0:T(8,128)(2,1)S(1)} async-done(((bf16[128,8,128]{2,1,0:T(8,128)(2,1)}), bf16[128,8,128]{2,1,0:T(8,128)(2,1)S(1)}, u32[]{:S(2)}, u32[]{:S(2)}) %all-to-all-start.1) | async-done | bytes 262176 | tf_op jit(solution)/shard_map/all_to_all | solution.py:120
  73.7 187.1 %while.21 = (s32[]{:T(128)}, f32[128,512]{1,0:T(8,128)}, f32[9,8,128]{2,1,0:T(8,128)}, f32[8,128,128]{2,0,1:T(8,128)}, s32[4]{0:T(128)S(1)}, /*index=5*/s32[4]{0...) while((s32[]{:T(128)}, f32[128,512]{1,0:T(8,128)}, ...), condition=%wide.region_13.14_spmd.clone.clone, body=%wide.region_0.13_spmd.clone.clone.sunk | while | flops 448201472 | bytes 62394652 | solution.py:110
  89.3 2.2 exponential_multiply_fusion.2
  107.0 3.4 fusion.167
  114.7 2.3 fusion.168
  135.2 2.2 exponential_multiply_fusion.2
  147.6 2.3 convolution_add_fusion.8
  154.0 3.4 fusion.167
  161.7 2.3 fusion.168
  182.3 2.2 exponential_multiply_fusion.2
  194.7 2.3 convolution_add_fusion.8
  201.1 3.4 fusion.167
  208.8 2.3 fusion.168
  229.3 2.2 exponential_multiply_fusion.2
  237.1 1.8 fusion.171
  241.7 2.3 convolution_add_fusion.8
  248.1 3.4 fusion.167
  255.8 2.3 fusion.168
  260.8 1.9 copy.80
  262.7 6.5 %all-to-all-start.2 = ((f32[128,8,128]{2,1,0:T(8,128)}), f32[128,8,128]{2,1,0:T(8,128)S(1)}, u32[]{:S(2)}, u32[]{:S(2)}) async-start(f32[128,8,128]{2,1,0:T(8,128)} %bitcast.11), calls=%async_computation.2 | async-start | bytes 1048576 | tf_op jit(solution)/shard_map/all_to_all | solution.py:132
  270.0 19.5 %all-to-all-done.2 = f32[128,8,128]{2,1,0:T(8,128)S(1)} async-done(((f32[128,8,128]{2,1,0:T(8,128)}), f32[128,8,128]{2,1,0:T(8,128)S(1)}, u32[]{:S(2)}, u32[]{:S(2)}) %all-to-all-start.2) | async-done | bytes 524320 | tf_op jit(solution)/shard_map/all_to_all | solution.py:132
  289.5 4.0 scatter_custom_fusion
  295.4 6.4 %all-to-all-start.3 = ((f32[9,128,8]{0,2,1:T(8,128)}), f32[9,128,8]{0,2,1:T(8,128)S(1)}, u32[]{:S(2)}, u32[]{:S(2)}) async-start(f32[9,128,8]{0,2,1:T(8,128)} %bitcast.13), calls=%async_computation.3 | async-start | bytes 1048576 | tf_op jit(solution)/shard_map/all_to_all | solution.py:131
  301.7 20.4 %all-to-all-done.3 = f32[9,128,8]{0,2,1:T(8,128)S(1)} async-done(((f32[9,128,8]{0,2,1:T(8,128)}), f32[9,128,8]{0,2,1:T(8,128)S(1)}, u32[]{:S(2)}, u32[]{:S(2)}) %all-to-all-start.3) | async-done | bytes 36896 | tf_op jit(solution)/shard_map/all_to_all | solution.py:131
  322.2 3.4 scatter_custom_fusion.1
  326.4 222.5 %all-reduce.14.cloned.1.call-done = f32[128,512]{1,0:T(8,128)} async-done(((f32[128,512]{1,0:T(8,128)}), f32[128,512]{1,0:T(8,128)}) %all-reduce.14.cloned.1.call-update) | async-done | bytes 262160 | tf_op jit(solution)/shard_map/psum | solution.py:139
  550.5 51.4 %all-reduce.12.cloned.1.call-done = f32[1024,128]{1,0:T(8,128)} async-done(((f32[1024,128]{1,0:T(8,128)}), f32[1024,128]{1,0:T(8,128)}) %all-reduce.12.cloned.1.call-update) | async-done | bytes 524304 | tf_op jit(solution)/shard_map/psum | solution.py:136
  (517 shorter events, 140.9 us)
Async XLA Ops:
  7.2 24.3 %copy-start = (bf16[1024,128]{1,0:T(8,128)(2,1)S(1)}, bf16[1024,128]{1,0:T(8,128)(2,1)}, u32[]{:S(2)}) copy-start(bf16[1024,128]{1,0:T(8,128)(2,1)} %param.10) | copy-start | bytes 786436
  14.1 37.7 %all-to-all-start = ((f32[9,128,8]{0,2,1:T(8,128)}), f32[9,128,8]{0,2,1:T(8,128)S(1)}, u32[]{:S(2)}, u32[]{:S(2)}) async-start(f32[9,128,8]{0,2,1:T(8,128)} %bitcast_select_fusion.1), calls=%async_computation | async-start | bytes 1048576 | tf_op jit(solution)/shard_map/all_to_all | solution.py:118
  51.8 21.3 %all-to-all-start.1 = ((bf16[128,8,128]{2,1,0:T(8,128)(2,1)}), bf16[128,8,128]{2,1,0:T(8,128)(2,1)S(1)}, u32[]{:S(2)}, u32[]{:S(2)}) async-start(bf16[128,8,128]{2,1,0:T(8,128)(2,1)} %bitcast_select_fusion.2), calls=%async_computation.1 | async-start | bytes 524288 | tf_op jit(solution)/shard_map/all_to_all | solution.py:120
  73.7 13.7 %copy-start.8 = (bf16[8,128,128]{2,1,0:T(8,128)(2,1)}, bf16[8,128,128]{2,1,0:T(8,128)(2,1)S(1)}, u32[]{:S(2)}) copy-start(bf16[8,128,128]{2,1,0:T(8,128)(2,1)S(1)} %get-tuple-element.843) | copy-start | bytes 786436 | tf_op jit(solution)/shard_map/while
  81.3 22.9 %copy-start.21 = (f32[256]{0:T(256)}, f32[256]{0:T(256)S(1)}, u32[]{:S(2)}) copy-start(f32[256]{0:T(256)S(1)} %get-tuple-element.768) | copy-start | bytes 3076 | tf_op jit(solution)/shard_map/while
  81.3 22.9 %copy-start.23 = (f32[256]{0:T(256)}, f32[256]{0:T(256)S(1)}, u32[]{:S(2)}) copy-start(f32[256]{0:T(256)S(1)} %get-tuple-element.765) | copy-start | bytes 3076 | tf_op jit(solution)/shard_map/while
  82.0 19.6 %copy-start.28 = (s32[8]{0:T(128)}, s32[8]{0:T(128)S(1)}, u32[]{:S(2)}) copy-start(s32[8]{0:T(128)S(1)} %get-tuple-element.785) | copy-start | bytes 100 | tf_op jit(solution)/shard_map/while
  84.2 18.9 %copy-start.5 = (f32[9,8,128]{2,0,1:T(8,128)}, f32[9,8,128]{2,0,1:T(8,128)S(1)}, u32[]{:S(2)}) copy-start(f32[9,8,128]{2,0,1:T(8,128)S(1)} %select_bitcast_fusion.2) | copy-start | bytes 110596 | tf_op jit(solution)/shard_map/while
  84.9 19.4 %copy-start.11 = (f32[1,8,128]{2,0,1:T(1,128)}, f32[1,8,128]{2,0,1:T(1,128)S(1)}, u32[]{:S(2)}) copy-start(f32[1,8,128]{2,0,1:T(1,128)S(1)} %get-tuple-element.769) | copy-start | bytes 12292 | tf_op jit(solution)/shard_map/while
  85.5 18.8 %copy-start.16 = (f32[1024]{0:T(1024)}, f32[1024]{0:T(1024)S(1)}, u32[]{:S(2)}) copy-start(f32[1024]{0:T(1024)S(1)} %bitcast_multiply_fusion.8) | copy-start | bytes 12292 | tf_op jit(solution)/shard_map/while
  127.3 24.0 %copy-start.21 = (f32[256]{0:T(256)}, f32[256]{0:T(256)S(1)}, u32[]{:S(2)}) copy-start(f32[256]{0:T(256)S(1)} %get-tuple-element.768) | copy-start | bytes 3076 | tf_op jit(solution)/shard_map/while
  127.3 24.0 %copy-start.23 = (f32[256]{0:T(256)}, f32[256]{0:T(256)S(1)}, u32[]{:S(2)}) copy-start(f32[256]{0:T(256)S(1)} %get-tuple-element.765) | copy-start | bytes 3076 | tf_op jit(solution)/shard_map/while
  128.0 19.6 %copy-start.28 = (s32[8]{0:T(128)}, s32[8]{0:T(128)S(1)}, u32[]{:S(2)}) copy-start(s32[8]{0:T(128)S(1)} %get-tuple-element.785) | copy-start | bytes 100 | tf_op jit(solution)/shard_map/while
  130.2 20.0 %copy-start.5 = (f32[9,8,128]{2,0,1:T(8,128)}, f32[9,8,128]{2,0,1:T(8,128)S(1)}, u32[]{:S(2)}) copy-start(f32[9,8,128]{2,0,1:T(8,128)S(1)} %select_bitcast_fusion.2) | copy-start | bytes 110596 | tf_op jit(solution)/shard_map/while
  130.8 20.5 %copy-start.11 = (f32[1,8,128]{2,0,1:T(1,128)}, f32[1,8,128]{2,0,1:T(1,128)S(1)}, u32[]{:S(2)}) copy-start(f32[1,8,128]{2,0,1:T(1,128)S(1)} %get-tuple-element.769) | copy-start | bytes 12292 | tf_op jit(solution)/shard_map/while
  131.4 19.9 %copy-start.16 = (f32[1024]{0:T(1024)}, f32[1024]{0:T(1024)S(1)}, u32[]{:S(2)}) copy-start(f32[1024]{0:T(1024)S(1)} %bitcast_multiply_fusion.8) | copy-start | bytes 12292 | tf_op jit(solution)/shard_map/while
  174.3 24.0 %copy-start.21 = (f32[256]{0:T(256)}, f32[256]{0:T(256)S(1)}, u32[]{:S(2)}) copy-start(f32[256]{0:T(256)S(1)} %get-tuple-element.768) | copy-start | bytes 3076 | tf_op jit(solution)/shard_map/while
  174.3 24.0 %copy-start.23 = (f32[256]{0:T(256)}, f32[256]{0:T(256)S(1)}, u32[]{:S(2)}) copy-start(f32[256]{0:T(256)S(1)} %get-tuple-element.765) | copy-start | bytes 3076 | tf_op jit(solution)/shard_map/while
  175.0 19.6 %copy-start.28 = (s32[8]{0:T(128)}, s32[8]{0:T(128)S(1)}, u32[]{:S(2)}) copy-start(s32[8]{0:T(128)S(1)} %get-tuple-element.785) | copy-start | bytes 100 | tf_op jit(solution)/shard_map/while
  177.2 20.0 %copy-start.5 = (f32[9,8,128]{2,0,1:T(8,128)}, f32[9,8,128]{2,0,1:T(8,128)S(1)}, u32[]{:S(2)}) copy-start(f32[9,8,128]{2,0,1:T(8,128)S(1)} %select_bitcast_fusion.2) | copy-start | bytes 110596 | tf_op jit(solution)/shard_map/while
  177.8 20.5 %copy-start.11 = (f32[1,8,128]{2,0,1:T(1,128)}, f32[1,8,128]{2,0,1:T(1,128)S(1)}, u32[]{:S(2)}) copy-start(f32[1,8,128]{2,0,1:T(1,128)S(1)} %get-tuple-element.769) | copy-start | bytes 12292 | tf_op jit(solution)/shard_map/while
  178.4 19.9 %copy-start.16 = (f32[1024]{0:T(1024)}, f32[1024]{0:T(1024)S(1)}, u32[]{:S(2)}) copy-start(f32[1024]{0:T(1024)S(1)} %bitcast_multiply_fusion.8) | copy-start | bytes 12292 | tf_op jit(solution)/shard_map/while
  221.3 24.0 %copy-start.21 = (f32[256]{0:T(256)}, f32[256]{0:T(256)S(1)}, u32[]{:S(2)}) copy-start(f32[256]{0:T(256)S(1)} %get-tuple-element.768) | copy-start | bytes 3076 | tf_op jit(solution)/shard_map/while
  221.3 24.0 %copy-start.23 = (f32[256]{0:T(256)}, f32[256]{0:T(256)S(1)}, u32[]{:S(2)}) copy-start(f32[256]{0:T(256)S(1)} %get-tuple-element.765) | copy-start | bytes 3076 | tf_op jit(solution)/shard_map/while
  222.0 19.6 %copy-start.28 = (s32[8]{0:T(128)}, s32[8]{0:T(128)S(1)}, u32[]{:S(2)}) copy-start(s32[8]{0:T(128)S(1)} %get-tuple-element.785) | copy-start | bytes 100 | tf_op jit(solution)/shard_map/while
  224.2 20.0 %copy-start.5 = (f32[9,8,128]{2,0,1:T(8,128)}, f32[9,8,128]{2,0,1:T(8,128)S(1)}, u32[]{:S(2)}) copy-start(f32[9,8,128]{2,0,1:T(8,128)S(1)} %select_bitcast_fusion.2) | copy-start | bytes 110596 | tf_op jit(solution)/shard_map/while
  224.9 20.5 %copy-start.11 = (f32[1,8,128]{2,0,1:T(1,128)}, f32[1,8,128]{2,0,1:T(1,128)S(1)}, u32[]{:S(2)}) copy-start(f32[1,8,128]{2,0,1:T(1,128)S(1)} %get-tuple-element.769) | copy-start | bytes 12292 | tf_op jit(solution)/shard_map/while
  225.5 19.9 %copy-start.16 = (f32[1024]{0:T(1024)}, f32[1024]{0:T(1024)S(1)}, u32[]{:S(2)}) copy-start(f32[1024]{0:T(1024)S(1)} %bitcast_multiply_fusion.8) | copy-start | bytes 12292 | tf_op jit(solution)/shard_map/while
  262.7 26.8 %all-to-all-start.2 = ((f32[128,8,128]{2,1,0:T(8,128)}), f32[128,8,128]{2,1,0:T(8,128)S(1)}, u32[]{:S(2)}, u32[]{:S(2)}) async-start(f32[128,8,128]{2,1,0:T(8,128)} %bitcast.11), calls=%async_computation.2 | async-start | bytes 1048576 | tf_op jit(solution)/shard_map/all_to_all | solution.py:132
  269.2 279.6 %all-reduce.14.cloned.1.call-start = ((), (), s32[]{:S(2)}) async-start(), calls=%async_computation.5 | async-start | bytes 524288 | tf_op jit(solution)/shard_map/psum | solution.py:139
  269.9 332.0 %all-reduce.12.cloned.1.call-start = ((), (), s32[]{:S(2)}) async-start(), calls=%async_computation.4 | async-start | bytes 1048576 | tf_op jit(solution)/shard_map/psum | solution.py:136
  295.4 26.8 %all-to-all-start.3 = ((f32[9,128,8]{0,2,1:T(8,128)}), f32[9,128,8]{0,2,1:T(8,128)S(1)}, u32[]{:S(2)}, u32[]{:S(2)}) async-start(f32[9,128,8]{0,2,1:T(8,128)} %bitcast.13), calls=%async_computation.3 | async-start | bytes 1048576 | tf_op jit(solution)/shard_map/all_to_all | solution.py:131
  (105 other events, 181.8 us)
Sparse Core Ops, SparseCore 0:
  275.6 273.1 all-reduce.13
  551.3 50.6 all-reduce.11
where the time goes:
time: 613 us; the launch traced here: 610 us
  waiting for transfers between devices  343 us (56%)
  local copies, waits for them, and re-layouts  79.9 us (13%)
  other arithmetic  76.6 us (12%)
  matrix products  39.1 us (6%)
  starting transfers between devices  36.8 us (6%)
  loops' own time  20.3 us (3%)
  between operations  14.3 us (2%)
    psum x1, waiting for transfers between devices, on_device(): lax.psum(decoder_sum, ('gs', 'view')) * (1.0 / math.sqrt(pixel_total))  222 us
    psum x1, waiting for transfers between devices, on_device(): summed = lax.psum(feat_own, 'view')  51.4 us
    another operation x8, other arithmetic, composite(): inner = jnp.cumsum(blocked, axis=2) - blocked  22.4 us
    all_to_all x1, waiting for transfers between devices, on_device(): lax.all_to_all(geo_acc, 'gs', split_axis=1, concat_axis=1, tiled=True)  20.4 us
    another operation x1, loops' own time, device_terms(): lax.scan(tile_step, start_totals, tile_range)  20.3 us
    all_to_all x1, waiting for transfers between devices, on_device(): lax.all_to_all(feat_acc, 'gs', split_axis=0, concat_axis=0, tiled=True)  19.5 us
    while x264, local copies, waits for them, and re-layouts  19.3 us
    all_to_all x1, starting transfers between devices, on_device(): lax.all_to_all(geo_send, 'gs', split_axis=1, concat_axis=1, tiled=True)  17.4 us
  transfers between devices with their start and end apart: 6, of which 6 were waited for; matrix products, arithmetic and copies ran while one was open for 3% of the time, Pallas kernels for 0%

commit v1 on v0

--- a/solution.py
+++ b/solution.py
@@ -136,7 +136,7 @@
     summed = lax.psum(feat_own, "view")
     feature_grad = lax.dynamic_slice_in_dim(summed, lax.axis_index("view") * quarter, quarter, 0)
     pixel_total = lax.axis_size("gs") * lax.axis_size("view") * tile_lists.shape[1] * TS * TS
-    decoder_grad = lax.psum(decoder_sum, ("gs", "view")) * (1.0 / math.sqrt(pixel_total))
+    decoder_grad = lax.psum(lax.psum(decoder_sum, "gs"), "view") * (1.0 / math.sqrt(pixel_total))
     return (feature_grad, geo_own[None], decoder_grad)
 
 

time: 613 us -> 532 us (0.87)
  waiting for transfers between devices: 343 us -> 258 us
    psum x1, waiting for transfers between devices: 222 us -> 170 us  [on_device(): lax.psum(decoder_sum, 'gs')]
    psum x1, waiting for transfers between devices: 51.4 us -> 18.5 us  [on_device(): summed = lax.psum(feat_own, 'view')]
where the time goes in v1:
time: 532 us; the launch traced here: 529 us
  waiting for transfers between devices  258 us (48%)
  local copies, waits for them, and re-layouts  80 us (15%)
  other arithmetic  76.6 us (14%)
  starting transfers between devices  41.1 us (8%)
  matrix products  39.3 us (7%)
  loops' own time  20.3 us (4%)
  between operations  14.3 us (3%)
    psum x1, waiting for transfers between devices, on_device(): lax.psum(decoder_sum, 'gs')  170 us
    another operation x8, other arithmetic, composite(): inner = jnp.cumsum(blocked, axis=2) - blocked  22.4 us
    another operation x1, loops' own time, device_terms(): lax.scan(tile_step, start_totals, tile_range)  20.3 us
    all_to_all x1, waiting for transfers between devices, on_device(): lax.all_to_all(geo_acc, 'gs', split_axis=1, concat_axis=1, tiled=True)  20.3 us
    all_to_all x1, waiting for transfers between devices, on_device(): lax.all_to_all(feat_acc, 'gs', split_axis=0, concat_axis=0, tiled=True)  19.5 us
    while x264, local copies, waits for them, and re-layouts  19.3 us
    psum x1, waiting for transfers between devices, on_device(): summed = lax.psum(feat_own, 'view')  18.5 us
    all_to_all x1, starting transfers between devices, on_device(): lax.all_to_all(geo_send, 'gs', split_axis=1, concat_axis=1, tiled=True)  17.4 us
  transfers between devices with their start and end apart: 6, of which 6 were waited for; matrix products, arithmetic and copies ran while one was open for 3% of the time, Pallas kernels for 0%

profile of v1, /device:TPU:8, one launch (start us, length us, event | category | flops | bytes accessed | tf_op | source)
XLA Modules:
  0.0 529.4 jit_solution(15248587001538018232)
XLA Ops:
  10.2 2.8 gather_fusion.2
  14.1 17.4 %all-to-all-start = ((f32[9,128,8]{0,2,1:T(8,128)}), f32[9,128,8]{0,2,1:T(8,128)S(1)}, u32[]{:S(2)}, u32[]{:S(2)}) async-start(f32[9,128,8]{0,2,1:T(8,128)} %bitcast_select_fusion.1), calls=%async_computation | async-start | bytes 1048576 | tf_op jit(solution)/shard_map/all_to_all | solution.py:118
  31.4 3.2 gather_fusion.3
  35.6 16.2 %all-to-all-done = f32[9,128,8]{0,2,1:T(8,128)S(1)} async-done(((f32[9,128,8]{0,2,1:T(8,128)}), f32[9,128,8]{0,2,1:T(8,128)S(1)}, u32[]{:S(2)}, u32[]{:S(2)}) %all-to-all-start) | async-done | bytes 36896 | tf_op jit(solution)/shard_map/all_to_all | solution.py:118
  51.7 6.5 %all-to-all-start.1 = ((bf16[128,8,128]{2,1,0:T(8,128)(2,1)}), bf16[128,8,128]{2,1,0:T(8,128)(2,1)S(1)}, u32[]{:S(2)}, u32[]{:S(2)}) async-start(bf16[128,8,128]{2,1,0:T(8,128)(2,1)} %bitcast_select_fusion.2), calls=%async_computation.1 | async-start | bytes 524288 | tf_op jit(solution)/shard_map/all_to_all | solution.py:120
  60.4 12.6 %all-to-all-done.1 = bf16[128,8,128]{2,1,0:T(8,128)(2,1)S(1)} async-done(((bf16[128,8,128]{2,1,0:T(8,128)(2,1)}), bf16[128,8,128]{2,1,0:T(8,128)(2,1)S(1)}, u32[]{:S(2)}, u32[]{:S(2)}) %all-to-all-start.1) | async-done | bytes 262176 | tf_op jit(solution)/shard_map/all_to_all | solution.py:120
  73.6 187.4 %while.21 = (s32[]{:T(128)}, f32[128,512]{1,0:T(8,128)}, f32[9,8,128]{2,1,0:T(8,128)}, f32[8,128,128]{2,0,1:T(8,128)}, s32[4]{0:T(128)S(1)}, /*index=5*/s32[4]{0...) while((s32[]{:T(128)}, f32[128,512]{1,0:T(8,128)}, ...), condition=%wide.region_13.14_spmd.clone.clone, body=%wide.region_0.13_spmd.clone.clone.sunk | while | flops 448201472 | bytes 62394652 | solution.py:110
  89.4 2.2 exponential_multiply_fusion.2
  97.2 1.8 fusion.171
  107.1 3.4 fusion.167
  114.7 2.3 fusion.168
  135.4 2.2 exponential_multiply_fusion.2
  147.8 2.3 convolution_add_fusion.8
  154.2 3.4 fusion.167
  161.8 2.3 fusion.168
  182.5 2.2 exponential_multiply_fusion.2
  194.9 2.3 convolution_add_fusion.8
  201.3 3.4 fusion.167
  208.9 2.3 fusion.168
  229.6 2.2 exponential_multiply_fusion.2
  242.0 2.3 convolution_add_fusion.8
  248.4 3.4 fusion.167
  256.0 2.3 fusion.168
  261.0 1.9 copy.80
  263.0 6.5 %all-to-all-start.2 = ((f32[128,8,128]{2,1,0:T(8,128)}), f32[128,8,128]{2,1,0:T(8,128)S(1)}, u32[]{:S(2)}, u32[]{:S(2)}) async-start(f32[128,8,128]{2,1,0:T(8,128)} %bitcast.11), calls=%async_computation.2 | async-start | bytes 1048576 | tf_op jit(solution)/shard_map/all_to_all | solution.py:132
  270.2 19.5 %all-to-all-done.2 = f32[128,8,128]{2,1,0:T(8,128)S(1)} async-done(((f32[128,8,128]{2,1,0:T(8,128)}), f32[128,8,128]{2,1,0:T(8,128)S(1)}, u32[]{:S(2)}, u32[]{:S(2)}) %all-to-all-start.2) | async-done | bytes 524320 | tf_op jit(solution)/shard_map/all_to_all | solution.py:132
  289.8 4.0 scatter_custom_fusion
  293.8 170.0 %all-reduce.13.cloned.1.call-done = f32[128,512]{1,0:T(8,128)} async-done(((f32[128,512]{1,0:T(8,128)}), f32[128,512]{1,0:T(8,128)}) %all-reduce.13.cloned.1.call-update) | async-done | bytes 262160 | tf_op jit(solution)/shard_map/psum | solution.py:139
  465.6 10.7 %all-to-all-start.3 = ((f32[9,128,8]{0,2,1:T(8,128)}), f32[9,128,8]{0,2,1:T(8,128)S(1)}, u32[]{:S(2)}, u32[]{:S(2)}) async-start(f32[9,128,8]{0,2,1:T(8,128)} %bitcast.13), calls=%async_computation.3 | async-start | bytes 1048576 | tf_op jit(solution)/shard_map/all_to_all | solution.py:131
  476.3 20.3 %all-to-all-done.3 = f32[9,128,8]{0,2,1:T(8,128)S(1)} async-done(((f32[9,128,8]{0,2,1:T(8,128)}), f32[9,128,8]{0,2,1:T(8,128)S(1)}, u32[]{:S(2)}, u32[]{:S(2)}) %all-to-all-start.3) | async-done | bytes 36896 | tf_op jit(solution)/shard_map/all_to_all | solution.py:131
  496.6 3.4 scatter_custom_fusion.1
  500.8 18.5 %all-reduce.15.cloned.1.call-done = (f32[1024,128]{1,0:T(8,128)}, f32[128,512]{1,0:T(8,128)}) async-done(((f32[1024,128]{1,0:T(8,128)}, f32[128,512]{1,0:T(8,128)}), (f32[1024,128]{1,0:T(8,128)}, f32[128,512]{1,0:T(8,128)})) %all-reduce.15.cloned.1.call-update) | async-done | bytes 786448 | tf_op jit(solution)/shard_map/psum | solution.py:136
  (517 shorter events, 141.1 us)
Async XLA Ops:
  7.2 24.3 %copy-start = (bf16[1024,128]{1,0:T(8,128)(2,1)S(1)}, bf16[1024,128]{1,0:T(8,128)(2,1)}, u32[]{:S(2)}) copy-start(bf16[1024,128]{1,0:T(8,128)(2,1)} %param.10) | copy-start | bytes 786436
  14.1 37.7 %all-to-all-start = ((f32[9,128,8]{0,2,1:T(8,128)}), f32[9,128,8]{0,2,1:T(8,128)S(1)}, u32[]{:S(2)}, u32[]{:S(2)}) async-start(f32[9,128,8]{0,2,1:T(8,128)} %bitcast_select_fusion.1), calls=%async_computation | async-start | bytes 1048576 | tf_op jit(solution)/shard_map/all_to_all | solution.py:118
  51.7 21.2 %all-to-all-start.1 = ((bf16[128,8,128]{2,1,0:T(8,128)(2,1)}), bf16[128,8,128]{2,1,0:T(8,128)(2,1)S(1)}, u32[]{:S(2)}, u32[]{:S(2)}) async-start(bf16[128,8,128]{2,1,0:T(8,128)(2,1)} %bitcast_select_fusion.2), calls=%async_computation.1 | async-start | bytes 524288 | tf_op jit(solution)/shard_map/all_to_all | solution.py:120
  73.7 13.7 %copy-start.8 = (bf16[8,128,128]{2,1,0:T(8,128)(2,1)}, bf16[8,128,128]{2,1,0:T(8,128)(2,1)S(1)}, u32[]{:S(2)}) copy-start(bf16[8,128,128]{2,1,0:T(8,128)(2,1)S(1)} %get-tuple-element.845) | copy-start | bytes 786436 | tf_op jit(solution)/shard_map/while
  81.4 23.0 %copy-start.21 = (f32[256]{0:T(256)}, f32[256]{0:T(256)S(1)}, u32[]{:S(2)}) copy-start(f32[256]{0:T(256)S(1)} %get-tuple-element.770) | copy-start | bytes 3076 | tf_op jit(solution)/shard_map/while
  81.4 23.0 %copy-start.23 = (f32[256]{0:T(256)}, f32[256]{0:T(256)S(1)}, u32[]{:S(2)}) copy-start(f32[256]{0:T(256)S(1)} %get-tuple-element.767) | copy-start | bytes 3076 | tf_op jit(solution)/shard_map/while
  82.1 19.6 %copy-start.28 = (s32[8]{0:T(128)}, s32[8]{0:T(128)S(1)}, u32[]{:S(2)}) copy-start(s32[8]{0:T(128)S(1)} %get-tuple-element.787) | copy-start | bytes 100 | tf_op jit(solution)/shard_map/while
  84.3 19.0 %copy-start.5 = (f32[9,8,128]{2,0,1:T(8,128)}, f32[9,8,128]{2,0,1:T(8,128)S(1)}, u32[]{:S(2)}) copy-start(f32[9,8,128]{2,0,1:T(8,128)S(1)} %select_bitcast_fusion.2) | copy-start | bytes 110596 | tf_op jit(solution)/shard_map/while
  84.9 19.4 %copy-start.11 = (f32[1,8,128]{2,0,1:T(1,128)}, f32[1,8,128]{2,0,1:T(1,128)S(1)}, u32[]{:S(2)}) copy-start(f32[1,8,128]{2,0,1:T(1,128)S(1)} %get-tuple-element.771) | copy-start | bytes 12292 | tf_op jit(solution)/shard_map/while
  85.5 18.9 %copy-start.16 = (f32[1024]{0:T(1024)}, f32[1024]{0:T(1024)S(1)}, u32[]{:S(2)}) copy-start(f32[1024]{0:T(1024)S(1)} %bitcast_multiply_fusion.8) | copy-start | bytes 12292 | tf_op jit(solution)/shard_map/while
  127.4 24.1 %copy-start.21 = (f32[256]{0:T(256)}, f32[256]{0:T(256)S(1)}, u32[]{:S(2)}) copy-start(f32[256]{0:T(256)S(1)} %get-tuple-element.770) | copy-start | bytes 3076 | tf_op jit(solution)/shard_map/while
  127.4 24.1 %copy-start.23 = (f32[256]{0:T(256)}, f32[256]{0:T(256)S(1)}, u32[]{:S(2)}) copy-start(f32[256]{0:T(256)S(1)} %get-tuple-element.767) | copy-start | bytes 3076 | tf_op jit(solution)/shard_map/while
  128.1 19.7 %copy-start.28 = (s32[8]{0:T(128)}, s32[8]{0:T(128)S(1)}, u32[]{:S(2)}) copy-start(s32[8]{0:T(128)S(1)} %get-tuple-element.787) | copy-start | bytes 100 | tf_op jit(solution)/shard_map/while
  130.3 20.1 %copy-start.5 = (f32[9,8,128]{2,0,1:T(8,128)}, f32[9,8,128]{2,0,1:T(8,128)S(1)}, u32[]{:S(2)}) copy-start(f32[9,8,128]{2,0,1:T(8,128)S(1)} %select_bitcast_fusion.2) | copy-start | bytes 110596 | tf_op jit(solution)/shard_map/while
  130.9 20.5 %copy-start.11 = (f32[1,8,128]{2,0,1:T(1,128)}, f32[1,8,128]{2,0,1:T(1,128)S(1)}, u32[]{:S(2)}) copy-start(f32[1,8,128]{2,0,1:T(1,128)S(1)} %get-tuple-element.771) | copy-start | bytes 12292 | tf_op jit(solution)/shard_map/while
  131.5 19.9 %copy-start.16 = (f32[1024]{0:T(1024)}, f32[1024]{0:T(1024)S(1)}, u32[]{:S(2)}) copy-start(f32[1024]{0:T(1024)S(1)} %bitcast_multiply_fusion.8) | copy-start | bytes 12292 | tf_op jit(solution)/shard_map/while
  174.5 24.1 %copy-start.21 = (f32[256]{0:T(256)}, f32[256]{0:T(256)S(1)}, u32[]{:S(2)}) copy-start(f32[256]{0:T(256)S(1)} %get-tuple-element.770) | copy-start | bytes 3076 | tf_op jit(solution)/shard_map/while
  174.5 24.1 %copy-start.23 = (f32[256]{0:T(256)}, f32[256]{0:T(256)S(1)}, u32[]{:S(2)}) copy-start(f32[256]{0:T(256)S(1)} %get-tuple-element.767) | copy-start | bytes 3076 | tf_op jit(solution)/shard_map/while
  175.2 19.7 %copy-start.28 = (s32[8]{0:T(128)}, s32[8]{0:T(128)S(1)}, u32[]{:S(2)}) copy-start(s32[8]{0:T(128)S(1)} %get-tuple-element.787) | copy-start | bytes 100 | tf_op jit(solution)/shard_map/while
  177.4 20.1 %copy-start.5 = (f32[9,8,128]{2,0,1:T(8,128)}, f32[9,8,128]{2,0,1:T(8,128)S(1)}, u32[]{:S(2)}) copy-start(f32[9,8,128]{2,0,1:T(8,128)S(1)} %select_bitcast_fusion.2) | copy-start | bytes 110596 | tf_op jit(solution)/shard_map/while
  178.0 20.5 %copy-start.11 = (f32[1,8,128]{2,0,1:T(1,128)}, f32[1,8,128]{2,0,1:T(1,128)S(1)}, u32[]{:S(2)}) copy-start(f32[1,8,128]{2,0,1:T(1,128)S(1)} %get-tuple-element.771) | copy-start | bytes 12292 | tf_op jit(solution)/shard_map/while
  178.6 20.0 %copy-start.16 = (f32[1024]{0:T(1024)}, f32[1024]{0:T(1024)S(1)}, u32[]{:S(2)}) copy-start(f32[1024]{0:T(1024)S(1)} %bitcast_multiply_fusion.8) | copy-start | bytes 12292 | tf_op jit(solution)/shard_map/while
  221.6 24.1 %copy-start.21 = (f32[256]{0:T(256)}, f32[256]{0:T(256)S(1)}, u32[]{:S(2)}) copy-start(f32[256]{0:T(256)S(1)} %get-tuple-element.770) | copy-start | bytes 3076 | tf_op jit(solution)/shard_map/while
  221.6 24.1 %copy-start.23 = (f32[256]{0:T(256)}, f32[256]{0:T(256)S(1)}, u32[]{:S(2)}) copy-start(f32[256]{0:T(256)S(1)} %get-tuple-element.767) | copy-start | bytes 3076 | tf_op jit(solution)/shard_map/while
  222.3 19.7 %copy-start.28 = (s32[8]{0:T(128)}, s32[8]{0:T(128)S(1)}, u32[]{:S(2)}) copy-start(s32[8]{0:T(128)S(1)} %get-tuple-element.787) | copy-start | bytes 100 | tf_op jit(solution)/shard_map/while
  224.5 20.1 %copy-start.5 = (f32[9,8,128]{2,0,1:T(8,128)}, f32[9,8,128]{2,0,1:T(8,128)S(1)}, u32[]{:S(2)}) copy-start(f32[9,8,128]{2,0,1:T(8,128)S(1)} %select_bitcast_fusion.2) | copy-start | bytes 110596 | tf_op jit(solution)/shard_map/while
  225.1 20.5 %copy-start.11 = (f32[1,8,128]{2,0,1:T(1,128)}, f32[1,8,128]{2,0,1:T(1,128)S(1)}, u32[]{:S(2)}) copy-start(f32[1,8,128]{2,0,1:T(1,128)S(1)} %get-tuple-element.771) | copy-start | bytes 12292 | tf_op jit(solution)/shard_map/while
  225.7 20.0 %copy-start.16 = (f32[1024]{0:T(1024)}, f32[1024]{0:T(1024)S(1)}, u32[]{:S(2)}) copy-start(f32[1024]{0:T(1024)S(1)} %bitcast_multiply_fusion.8) | copy-start | bytes 12292 | tf_op jit(solution)/shard_map/while
  263.0 26.8 %all-to-all-start.2 = ((f32[128,8,128]{2,1,0:T(8,128)}), f32[128,8,128]{2,1,0:T(8,128)S(1)}, u32[]{:S(2)}, u32[]{:S(2)}) async-start(f32[128,8,128]{2,1,0:T(8,128)} %bitcast.11), calls=%async_computation.2 | async-start | bytes 1048576 | tf_op jit(solution)/shard_map/all_to_all | solution.py:132
  269.4 194.3 %all-reduce.13.cloned.1.call-start = ((), (), s32[]{:S(2)}) async-start(), calls=%async_computation.4 | async-start | bytes 524288 | tf_op jit(solution)/shard_map/psum | solution.py:139
  270.2 249.1 %all-reduce.15.cloned.1.call-start = ((), (), s32[]{:S(2)}) async-start(), calls=%async_computation.5 | async-start | bytes 1572864 | tf_op jit(solution)/shard_map/psum | solution.py:136
  465.6 31.0 %all-to-all-start.3 = ((f32[9,128,8]{0,2,1:T(8,128)}), f32[9,128,8]{0,2,1:T(8,128)S(1)}, u32[]{:S(2)}, u32[]{:S(2)}) async-start(f32[9,128,8]{0,2,1:T(8,128)} %bitcast.13), calls=%async_computation.3 | async-start | bytes 1048576 | tf_op jit(solution)/shard_map/all_to_all | solution.py:131
  (105 other events, 182.3 us)
Sparse Core Ops, SparseCore 0:
  274.1 189.6 all-reduce.12
  466.3 52.9 all-reduce.14
